TPU v7x, 256 devices: a whole 4x4x8 slice. The times are simulated.
256 devices in a mesh: pipe: 2 (over core), obs: 16 (over y, x), patch: 8 (over z).
Axes of the slice: x: 4, y: 4, z: 8, core: 2. Of those that a mesh axis runs over, the one named last changes fastest.
Arguments:
- patch_tokens: bfloat16 [4096, 2048], P('patch', 'obs'), may hold values from -40 to 40
- obs_tokens: bfloat16 [2048, 2048], P('patch', 'obs'), may hold values from -40 to 40
- footprint: int32 [32, 8], P('patch'), may hold values from 0 to 15, as said below
- list_counts: int32 [32], P('patch'), may hold values from 1 to 8
- footprint_bias: float32 [32, 8], P('patch'), may hold values from -4 to 290
- w_query: bfloat16 [2, 2048, 2048], P('pipe', None, 'obs'), may hold values from -0.125 to 0.125
- w_key: bfloat16 [2, 2048, 2048], P('pipe', None, 'obs'), may hold values from -0.125 to 0.125
- w_value: bfloat16 [2, 2048, 2048], P('pipe', None, 'obs'), may hold values from -0.125 to 0.125
- w_out: bfloat16 [2, 2048, 2048], P('pipe', 'obs'), may hold values from -0.125 to 0.125
- patch_gain: float32 [2, 2048], P('pipe'), may hold values from 0.1 to 1.9
- obs_gain: float32 [2, 2048], P('pipe'), may hold values from 0.1 to 1.9
Outputs:
- sections: bfloat16 [2, 4096, 2048], P('pipe', 'patch', 'obs')
Inputs may be any that keep to these rules, and one draw needn't show every extreme that they name: `footprint`: entries are global observation block indices. In each row the first list_counts entries (the live ones) are distinct, the rest are to be ignored. For a device along patch and any device along patch, all live entries of the first device's rows that lie in the second device's range of 2 blocks name one and the same block.
All inputs are finite; a program needn't handle non-finite values.
Results may differ from a plain program's by a relative error of at most 0.012.
Values may be sent and summed in bfloat16 or wider, within the bound.
No kernel may reach another device: no remote copies, remote signals or barrier semaphores. Data moves between devices by JAX's collectives and lax.ppermute only.
A program may use at most 64 MiB of HBM per device.

v0:
```python
import jax
import jax.numpy as jnp
from jax import lax
from jax.sharding import PartitionSpec as P

HS = 128
BLK = 128
MB = 128


def passed_along(value, axis, steps):
    count = lax.axis_size(axis)
    first, last = (max(0, -steps), min(count, count - steps))
    return lax.ppermute(value, axis, [(source, source + steps) for source in range(first, last)])


def rms_round(values, gain):
    widened = values.astype(jnp.float32)
    scaled = widened * lax.rsqrt(jnp.mean(widened * widened, axis=-1, keepdims=True) + 1e-05)
    return (scaled * gain).astype(jnp.bfloat16)


def store_rows(sections, out_piece, is_valid, row_start):
    current = lax.dynamic_slice_in_dim(sections, row_start, out_piece.shape[0], 1)
    kept = jnp.where(is_valid, out_piece[None], current)
    return lax.dynamic_update_slice_in_dim(sections, kept, row_start, 1)


def on_device(
    patch_tokens,
    obs_tokens,
    footprint,
    list_counts,
    footprint_bias,
    w_query,
    w_key,
    w_value,
    w_out,
    patch_gain,
    obs_gain,
):
    pipe_segment = lax.axis_index("pipe")
    segment_count = lax.axis_size("pipe")
    obs_column = lax.axis_index("obs")
    feature_part = patch_tokens.shape[1]
    full_features = feature_part * lax.axis_size("obs")
    head_width = w_query.shape[2]
    heads_here = head_width // HS
    list_slots = footprint.shape[1]
    micro_count = patch_tokens.shape[0] // MB
    blocks_micro = MB // BLK
    score_scale = HS ** (-0.5)
    observed = lax.all_gather(obs_tokens, "obs", axis=1, tiled=True)
    obs_normed = rms_round(observed, obs_gain[0])
    key_values = jnp.concatenate(
        [
            jnp.dot(obs_normed, w_key[0], preferred_element_type=jnp.float32).astype(jnp.bfloat16),
            jnp.dot(obs_normed, w_value[0], preferred_element_type=jnp.float32).astype(
                jnp.bfloat16
            ),
        ],
        axis=1,
    )
    local_blocks = key_values.reshape(-1, BLK, 2 * head_width)
    kv_table = lax.all_gather(local_blocks, "patch", axis=0, tiled=True)

    def attend_block(segment_input, micro_index):
        patch_normed = rms_round(segment_input, patch_gain[0])
        queries = (
            jnp.dot(patch_normed, w_query[0], preferred_element_type=jnp.float32) * score_scale
        ).astype(jnp.bfloat16)
        queries = queries.reshape(blocks_micro, BLK, heads_here, HS)
        first_block = micro_index * blocks_micro
        slot_part = lax.dynamic_slice_in_dim(footprint, first_block, blocks_micro, 0)
        count_part = lax.dynamic_slice_in_dim(list_counts, first_block, blocks_micro, 0)
        bias_part = lax.dynamic_slice_in_dim(footprint_bias, first_block, blocks_micro, 0)
        picked = kv_table[slot_part].reshape(blocks_micro, list_slots * BLK, 2 * head_width)
        key_part = picked[:, :, :head_width].reshape(blocks_micro, list_slots * BLK, heads_here, HS)
        value_part = picked[:, :, head_width:].reshape(
            blocks_micro, list_slots * BLK, heads_here, HS
        )
        scores = jnp.einsum(
            "bqhd,bkhd->bhqk", queries, key_part, preferred_element_type=jnp.float32
        )
        alive_mask = jnp.repeat(jnp.arange(list_slots)[None, :] < count_part[:, None], BLK, axis=1)
        added = jnp.repeat(bias_part, BLK, axis=1)
        scores = jnp.where(alive_mask[:, None, None, :], scores + added[:, None, None, :], -1e30)
        row_max = jnp.max(scores, axis=-1, keepdims=True)
        weights = jnp.exp(scores - row_max)
        weights = (weights / jnp.sum(weights, axis=-1, keepdims=True)).astype(jnp.bfloat16)
        context = jnp.einsum(
            "bhqk,bkhd->bqhd", weights, value_part, preferred_element_type=jnp.float32
        ).astype(jnp.bfloat16)
        context = context.reshape(MB, head_width)
        return jnp.dot(context, w_out[0], preferred_element_type=jnp.float32)

    def spare_block(segment_input, micro_index):
        return jnp.zeros((MB, full_features), jnp.float32)

    tick_total = micro_count + segment_count - 1
    sections = jnp.zeros((1, patch_tokens.shape[0], feature_part), jnp.bfloat16)
    rows_all = lax.all_gather(patch_tokens, "obs", axis=1, tiled=True)
    arriving = jnp.zeros((MB, full_features), jnp.bfloat16)
    for tick_num in range(tick_total):
        tick_micro = tick_num - pipe_segment
        is_valid = (tick_micro >= 0) & (tick_micro < micro_count)
        micro_index = jnp.clip(tick_micro, 0, micro_count - 1)
        own_rows = lax.dynamic_slice_in_dim(rows_all, micro_index * MB, MB, 0)
        segment_input = jnp.where(pipe_segment == 0, own_rows, arriving)
        partial_value = lax.cond(is_valid, attend_block, spare_block, segment_input, micro_index)
        head_total = lax.psum(partial_value.astype(jnp.bfloat16), "obs").astype(jnp.float32)
        segment_output = (segment_input.astype(jnp.float32) + head_total).astype(jnp.bfloat16)
        out_piece = lax.dynamic_slice_in_dim(
            segment_output, obs_column * feature_part, feature_part, 1
        )
        sections = store_rows(sections, out_piece, is_valid, micro_index * MB)
        if tick_num + 1 < tick_total:
            arriving = passed_along(segment_output, "pipe", 1)
    return sections


def solution(mesh):
    in_specs = (
        P("patch", "obs"),
        P("patch", "obs"),
        P("patch", None),
        P("patch"),
        P("patch", None),
        P("pipe", None, "obs"),
        P("pipe", None, "obs"),
        P("pipe", None, "obs"),
        P("pipe", "obs", None),
        P("pipe", None),
        P("pipe", None),
    )
    out_specs = P("pipe", "patch", "obs")
    return jax.shard_map(
        on_device, mesh=mesh, in_specs=in_specs, out_specs=out_specs, check_vma=False
    )
```

profile of v0, /device:TPU:2, one launch (start us, length us, event | category | flops | bytes accessed | tf_op | source)
XLA Modules:
  0.0 700.2 jit_solution(2485516238832570236)
XLA Ops:
  6.5 0.7 all-gather.6.cloned.1.call-update
  7.3 0.7 all-gather.4.cloned.1.call-update
  8.1 52.5 %all-gather.6.cloned.1.call-done = bf16[256,2048]{1,0:T(8,128)(2,1)} async-done(((bf16[256,128]{1,0:T(8,128)(2,1)}), bf16[256,2048]{1,0:T(8,128)(2,1)}) %all-gather.6.cloned.1.call-update) | async-done | bytes 1048592 | tf_op jit(solution)/shard_map/all_gather | solution.py:53
  60.6 1.6 fusion.120
  62.2 1.8 convolution_convert_fusion.5
  64.7 0.8 copy.14
  65.5 48.9 %all-gather.4.cloned.1.call-done = bf16[512,2048]{1,0:T(8,128)(2,1)} async-done(((bf16[512,128]{1,0:T(8,128)(2,1)}), bf16[512,2048]{1,0:T(8,128)(2,1)}) %all-gather.4.cloned.1.call-update) | async-done | bytes 2097168 | tf_op jit(solution)/shard_map/all_gather | solution.py:102
  114.4 1.1 dynamic-slice_select_fusion.4
  115.6 38.8 %all-gather.8.cloned.1.call-done = bf16[16,128,256]{2,1,0:T(8,128)(2,1)} async-done(((bf16[2,128,256]{2,1,0:T(8,128)(2,1)}), bf16[16,128,256]{2,1,0:T(8,128)(2,1)}) %all-gather.8.cloned.1.call-update) | async-done | bytes 1048592 | tf_op jit(solution)/shard_map/all_gather | solution.py:65
  154.4 6.1 conditional.5
  154.5 1.8 gather_fusion
  156.5 0.6 dynamic_slice.36
  157.1 0.6 iota_compare_fusion
  157.9 0.6 fusion.133
  158.7 1.8 fusion.3
  160.5 0.8 copy-done.2
  161.4 93.9 %all-reduce.6.cloned.1.call-done = bf16[128,2048]{1,0:T(8,128)(2,1)} async-done(((bf16[128,2048]{1,0:T(8,128)(2,1)}), bf16[128,2048]{1,0:T(8,128)(2,1)}) %all-reduce.6.cloned.1.call-update) | async-done | bytes 524304 | tf_op jit(solution)/shard_map/psum | solution.py:111
  255.3 2.1 add_convert_fusion.3
  257.5 1.3 collective-permute-start
  258.8 1.7 collective-permute-done
  260.5 1.2 dynamic-slice_select_fusion.3
  261.7 6.7 conditional.6
  261.7 0.8 copy-done.15
  262.5 0.6 gather_fusion.1
  263.3 0.6 dynamic_slice.70
  263.9 0.6 iota_compare_fusion.1
  264.6 1.6 fusion.138
  266.5 1.9 fusion.27
  268.4 0.8 copy-done.3
  269.3 95.4 %all-reduce.8.cloned.1.call-done = bf16[128,2048]{1,0:T(8,128)(2,1)} async-done(((bf16[128,2048]{1,0:T(8,128)(2,1)}), bf16[128,2048]{1,0:T(8,128)(2,1)}) %all-reduce.8.cloned.1.call-update) | async-done | bytes 524304 | tf_op jit(solution)/shard_map/psum | solution.py:111
  364.6 1.2 add_convert_fusion.2
  365.8 1.3 collective-permute-start.1
  367.1 1.5 collective-permute-done.1
  368.6 1.2 dynamic-slice_select_fusion.2
  369.8 7.7 %conditional.7 = (bf16[128,2048]{1,0:T(8,128)(2,1)S(1)}) conditional(s32[]{:T(128)} %convert_element_type.212, () %tuple.39, (s32[]{:T(128)}, s32[4,8]{1,0:T(4,128)S(1)}, bf16[16,128,256]{2,1,0:T(8,128)(2,1)S(1)}, s32[4]{0:T(128)S(1)}, bf16[128,2048]{1,0:T(8,128)(2,1)S(1)}, /*index=5*/f32[1,2048]{1,0:T(1,128)S(1)}, ...), branch_computations={%region_13.14_spmd, %region_14.18_spmd} | conditional | flops 204260256 | bytes 7891790 | solution.py:110
  369.9 1.4 gather_fusion.2
  371.5 0.6 dynamic_slice.74
  372.7 1.7 fusion.143
  374.4 0.8 copy-done.10
  375.4 2.0 fusion.51
  377.5 0.8 copy-done.4
  378.4 95.4 %all-reduce.10.cloned.1.call-done = bf16[128,2048]{1,0:T(8,128)(2,1)} async-done(((bf16[128,2048]{1,0:T(8,128)(2,1)}), bf16[128,2048]{1,0:T(8,128)(2,1)}) %all-reduce.10.cloned.1.call-update) | async-done | bytes 524304 | tf_op jit(solution)/shard_map/psum | solution.py:111
  473.7 1.2 add_convert_fusion.1
  474.9 2.1 collective-permute-start.2
  477.0 0.8 collective-permute-done.2
  477.9 1.2 dynamic-slice_select_fusion.1
  479.1 7.8 %conditional.8 = (bf16[128,2048]{1,0:T(8,128)(2,1)S(1)}) conditional(s32[]{:T(128)} %convert_element_type.217, () %tuple.41, (s32[]{:T(128)}, s32[4,8]{1,0:T(4,128)S(1)}, bf16[16,128,256]{2,1,0:T(8,128)(2,1)S(1)}, s32[4]{0:T(128)S(1)}, bf16[128,2048]{1,0:T(8,128)(2,1)S(1)}, /*index=5*/f32[1,2048]{1,0:T(1,128)S(1)}, ...), branch_computations={%region_19.20_spmd, %region_20.24_spmd} | conditional | flops 204260256 | bytes 7891790 | solution.py:110
  479.2 1.4 gather_fusion.3
  480.8 0.7 dynamic_slice.78
  481.4 0.6 iota_compare_fusion.3
  482.1 1.7 fusion.148
  483.9 0.8 copy-done.11
  484.9 2.0 fusion.75
  486.9 0.8 copy-done.5
  487.8 95.6 %all-reduce.12.cloned.1.call-done = bf16[128,2048]{1,0:T(8,128)(2,1)} async-done(((bf16[128,2048]{1,0:T(8,128)(2,1)}), bf16[128,2048]{1,0:T(8,128)(2,1)}) %all-reduce.12.cloned.1.call-update) | async-done | bytes 524304 | tf_op jit(solution)/shard_map/psum | solution.py:111
  583.3 1.2 add_convert_fusion
  584.5 2.1 collective-permute-start.3
  586.6 0.8 collective-permute-done.3
  587.5 1.2 dynamic-slice_select_fusion
  588.7 0.8 copy-done.6
  589.5 0.8 bitcast_dynamic-update-slice_fusion
  590.4 0.8 fusion.131
  591.2 100.7 %all-reduce.14.cloned.1.call-done = bf16[128,2048]{1,0:T(8,128)(2,1)} async-done(((bf16[128,2048]{1,0:T(8,128)(2,1)}), bf16[128,2048]{1,0:T(8,128)(2,1)}) %all-reduce.14.cloned.1.call-update) | async-done | bytes 524304 | tf_op jit(solution)/shard_map/psum | solution.py:111
  691.9 1.4 fusion.129
  (89 shorter events, 4.2 us)
Async XLA Ops:
  6.5 55.6 %copy-start = (bf16[1,2048,128]{2,1,0:T(8,128)(2,1)S(1)}, bf16[1,2048,128]{2,1,0:T(8,128)(2,1)}, u32[]{:S(2)}) copy-start(bf16[1,2048,128]{2,1,0:T(8,128)(2,1)} %param.28) | copy-start | bytes 1572868
  6.5 57.4 %copy-start.16 = (f32[1,2048]{1,0:T(1,128)S(1)}, f32[1,2048]{1,0:T(1,128)}, u32[]{:S(2)}) copy-start(f32[1,2048]{1,0:T(1,128)} %param.31) | copy-start | bytes 24580
  6.5 57.4 %copy-start.13 = (bf16[1,2048,128]{2,1,0:T(8,128)(2,1)S(1)}, bf16[1,2048,128]{2,1,0:T(8,128)(2,1)}, u32[]{:S(2)}) copy-start(bf16[1,2048,128]{2,1,0:T(8,128)(2,1)} %param.27) | copy-start | bytes 1572868
  6.5 54.0 %all-gather.6.cloned.1.call-start = ((), (), s32[]{:S(2)}) async-start(), calls=%async_computation.1 | async-start | bytes 1114112 | tf_op jit(solution)/shard_map/all_gather | solution.py:53
  7.3 107.2 %all-gather.4.cloned.1.call-start = ((), (), s32[]{:S(2)}) async-start(), calls=%async_computation | async-start | bytes 2228224 | tf_op jit(solution)/shard_map/all_gather | solution.py:102
  8.0 146.4 %all-gather.8.cloned.1.call-start = ((), (), s32[]{:S(2)}) async-start(), calls=%async_computation.2 | async-start | bytes 1179648 | tf_op jit(solution)/shard_map/all_gather | solution.py:65
  60.5 3.4 copy-start.7
  64.0 90.4 %copy-start.14 = (bf16[1,2048,128]{2,1,0:T(8,128)(2,1)S(1)}, bf16[1,2048,128]{2,1,0:T(8,128)(2,1)}, u32[]{:S(2)}) copy-start(bf16[1,2048,128]{2,1,0:T(8,128)(2,1)} %param.26) | copy-start | bytes 1572868
  64.0 90.4 %copy-start.17 = (f32[1,2048]{1,0:T(1,128)S(1)}, f32[1,2048]{1,0:T(1,128)}, u32[]{:S(2)}) copy-start(f32[1,2048]{1,0:T(1,128)} %param.30) | copy-start | bytes 24580
  64.0 90.4 %copy-start.18 = (s32[4,8]{1,0:T(4,128)S(1)}, s32[4,8]{1,0:T(4,128)}, u32[]{:S(2)}) copy-start(s32[4,8]{1,0:T(4,128)} %param.23) | copy-start | bytes 388
  64.0 90.4 %copy-start.19 = (f32[4,8]{1,0:T(4,128)S(1)}, f32[4,8]{1,0:T(4,128)}, u32[]{:S(2)}) copy-start(f32[4,8]{1,0:T(4,128)} %param.25) | copy-start | bytes 388
  64.0 90.3 %copy-start.20 = (s32[4]{0:T(128)S(1)}, s32[4]{0:T(128)}, u32[]{:S(2)}) copy-start(s32[4]{0:T(128)} %param.24) | copy-start | bytes 52
  65.4 189.9 %all-reduce.6.cloned.1.call-start = ((), (), s32[]{:S(2)}) async-start(), calls=%async_computation.3 | async-start | bytes 1048576 | tf_op jit(solution)/shard_map/psum | solution.py:111
  160.5 0.8 copy-start.2
  160.5 101.1 %copy-start.1 = (bf16[16,128,256]{2,1,0:T(8,128)(2,1)S(1)}, bf16[16,128,256]{2,1,0:T(8,128)(2,1)}, u32[]{:S(2)}) copy-start(bf16[16,128,256]{2,1,0:T(8,128)(2,1)} %all-gather.8.cloned.1.call-done) | copy-start | bytes 3145732
  161.3 203.3 %all-reduce.8.cloned.1.call-start = ((), (), s32[]{:S(2)}) async-start(), calls=%async_computation.4 | async-start | bytes 1048576 | tf_op jit(solution)/shard_map/psum | solution.py:111
  257.5 3.0 collective-permute-start
  261.7 0.8 copy-start.15
  263.1 3.1 copy-start.12
  268.4 0.8 copy-start.3
  269.2 204.5 %all-reduce.10.cloned.1.call-start = ((), (), s32[]{:S(2)}) async-start(), calls=%async_computation.5 | async-start | bytes 1048576 | tf_op jit(solution)/shard_map/psum | solution.py:111
  365.8 2.8 collective-permute-start.1
  374.4 0.8 copy-start.10
  377.5 0.8 copy-start.4
  378.3 205.0 %all-reduce.12.cloned.1.call-start = ((), (), s32[]{:S(2)}) async-start(), calls=%async_computation.6 | async-start | bytes 1048576 | tf_op jit(solution)/shard_map/psum | solution.py:111
  474.9 4.1 copy-start.8
  474.9 2.9 collective-permute-start.2
  483.8 0.8 copy-start.11
  486.9 0.8 copy-start.5
  487.7 204.2 %all-reduce.14.cloned.1.call-start = ((), (), s32[]{:S(2)}) async-start(), calls=%async_computation.7 | async-start | bytes 1048576 | tf_op jit(solution)/shard_map/psum | solution.py:111
  584.5 2.9 collective-permute-start.3
  588.7 0.8 copy-start.6
  591.2 100.7 %copy-start.9 = (bf16[1,512,128]{2,1,0:T(8,128)(2,1)}, bf16[1,512,128]{2,1,0:T(8,128)(2,1)S(1)}, u32[]{:S(2)}) copy-start(bf16[1,512,128]{2,1,0:T(8,128)(2,1)S(1)} %fusion.130) | copy-start | bytes 393220
Sparse Core Ops, SparseCore 0:
  9.7 50.7 all-gather.5
  63.0 51.4 all-gather.3
  116.2 38.1 all-gather.7
  161.4 93.8 all-reduce.5
  269.3 95.2 all-reduce.7
  378.4 95.2 all-reduce.9
  487.9 95.4 all-reduce.11
  589.6 102.2 all-reduce.13
where the time goes:
time: 701 us; the launch traced here: 700 us
  waiting for transfers between devices  628 us (90%)
  other arithmetic  20.3 us (3%)
  matrix products  15.8 us (2%)
  local copies, waits for them, and re-layouts  15.4 us (2%)
  between operations  13.8 us (2%)
  starting transfers between devices  7.12 us (1%)
    psum x5, waiting for transfers between devices, on_device(): lax.psum(partial_value.astype(jnp.bfloat16), 'obs').astype(jnp.float32)  481 us
    all_gather x1, waiting for transfers between devices, on_device(): observed = lax.all_gather(obs_tokens, 'obs', axis=1, tiled=True)  52.5 us
    all_gather x1, waiting for transfers between devices, on_device(): rows_all = lax.all_gather(patch_tokens, 'obs', axis=1, tiled=True)  48.9 us
    all_gather x1, waiting for transfers between devices, on_device(): kv_table = lax.all_gather(local_blocks, 'patch', axis=0, tiled=True)  38.8 us
  transfers between devices with their start and end apart: 12, of which 12 were waited for; matrix products, arithmetic and copies ran while one was open for 1% of the time, Pallas kernels for 0%

commit v1 on v0

--- a/solution.py
+++ b/solution.py
@@ -6,6 +6,22 @@
 HS = 128
 BLK = 128
 MB = 128
+
+
+def ring_gather(x, axis, dim):
+    ways, here, step = (lax.axis_size(axis), lax.axis_index(axis), x.shape[dim])
+    lengths = [n * ways if d == dim else n for d, n in enumerate(x.shape)]
+    full = lax.dynamic_update_slice_in_dim(jnp.zeros(lengths, x.dtype), x, here * step, axis=dim)
+    going_up = going_down = x
+    for far in range(1, ways // 2 + 1):
+        going_up = lax.ppermute(going_up, axis, [(d, (d + 1) % ways) for d in range(ways)])
+        full = lax.dynamic_update_slice_in_dim(full, going_up, (here - far) % ways * step, axis=dim)
+        if 2 * far < ways:
+            going_down = lax.ppermute(going_down, axis, [(d, (d - 1) % ways) for d in range(ways)])
+            full = lax.dynamic_update_slice_in_dim(
+                full, going_down, (here + far) % ways * step, axis=dim
+            )
+    return full
 
 
 def passed_along(value, axis, steps):
@@ -50,7 +66,7 @@
     micro_count = patch_tokens.shape[0] // MB
     blocks_micro = MB // BLK
     score_scale = HS ** (-0.5)
-    observed = lax.all_gather(obs_tokens, "obs", axis=1, tiled=True)
+    observed = ring_gather(obs_tokens, "obs", 1)
     obs_normed = rms_round(observed, obs_gain[0])
     key_values = jnp.concatenate(
         [

time: 701 us -> 655 us (0.934)
  waiting for transfers between devices: 628 us -> 549 us
  starting transfers between devices: 7.12 us -> 41.7 us
    all_gather x1 -> x0, waiting for transfers between devices: 52.5 us -> none  [on_device(): observed = lax.all_gather(obs_tokens, 'obs', axis=1, tiled=True)]
    all_gather x1, waiting for transfers between devices: 48.9 us -> 0.02 us  [on_device(): rows_all = lax.all_gather(patch_tokens, 'obs', axis=1, tiled=True)]
    ppermute x0 -> x15, starting transfers between devices: none -> 34.6 us  [the longest x7 31.7 us: ring_gather(): lax.ppermute(going_down, axis, [(d, (d - 1) % ways) for d in range(ways)])]
    ppermute x0 -> x15, waiting for transfers between devices: none -> 24.2 us  [the longest x8 24.2 us: ring_gather(): lax.ppermute(going_up, axis, [(d, (d + 1) % ways) for d in range(ways)])]
  transfers between devices with their start and end apart: 12 -> 26, of which waited for: 12 -> 18; matrix products, arithmetic and copies ran while one was open for 1% -> 1% of each run, Pallas kernels for 0% -> 0%
where the time goes in v1:
time: 655 us; the launch traced here: 653 us
  waiting for transfers between devices  549 us (84%)
  starting transfers between devices  41.7 us (6%)
  other arithmetic  18.1 us (3%)
  local copies, waits for them, and re-layouts  15.8 us (2%)
  matrix products  14.6 us (2%)
  between operations  13.9 us (2%)
    psum x5, waiting for transfers between devices, on_device(): lax.psum(partial_value.astype(jnp.bfloat16), 'obs').astype(jnp.float32)  481 us
    all_gather x1, waiting for transfers between devices, on_device(): kv_table = lax.all_gather(local_blocks, 'patch', axis=0, tiled=True)  38.7 us
    ppermute x7, starting transfers between devices, ring_gather(): lax.ppermute(going_down, axis, [(d, (d - 1) % ways) for d in range(ways)])  31.7 us
    ppermute x8, waiting for transfers between devices, ring_gather(): lax.ppermute(going_up, axis, [(d, (d + 1) % ways) for d in range(ways)])  24.2 us
  transfers between devices with their start and end apart: 26, of which 18 were waited for; matrix products, arithmetic and copies ran while one was open for 1% of the time, Pallas kernels for 0%

profile of v1, /device:TPU:2, one launch (start us, length us, event | category | flops | bytes accessed | tf_op | source)
XLA Modules:
  0.0 653.5 jit_solution(7598545366572140734)
XLA Ops:
  7.3 1.6 collective-permute-start
  8.9 0.8 collective-permute-start.1
  9.8 0.9 constant_dynamic-update-slice_fusion.15
  10.7 1.4 collective-permute-done
  12.1 1.3 collective-permute-start.2
  13.4 4.1 collective-permute-start.3
  17.5 2.2 collective-permute-done.2
  19.7 5.3 collective-permute-start.5
  25.1 2.6 collective-permute-done.4
  27.7 5.5 collective-permute-start.7
  33.2 2.8 collective-permute-done.6
  36.0 5.2 collective-permute-start.9
  41.2 2.2 collective-permute-done.8
  43.4 5.3 collective-permute-start.11
  48.8 3.3 collective-permute-done.10
  52.1 5.5 collective-permute-start.13
  57.7 2.5 collective-permute-done.12
  60.3 7.2 %collective-permute-done.14 = bf16[256,128]{1,0:T(8,128)(2,1)S(1)} collective-permute-done((bf16[256,128]{1,0:T(8,128)(2,1)S(1)}, bf16[256,128]{1,0:T(8,128)(2,1)S(1)}, u32[]{:S(2)}, u32[]{:S(2)}) %collective-permute-start.14) | collective-permute-done | bytes 65568 | tf_op jit(solution)/shard_map/ppermute | solution.py:17
  69.9 1.1 dynamic-slice_select_fusion.4
  71.1 38.7 %all-gather.5.cloned.1.call-done = bf16[16,128,256]{2,1,0:T(8,128)(2,1)} async-done(((bf16[2,128,256]{2,1,0:T(8,128)(2,1)}), bf16[16,128,256]{2,1,0:T(8,128)(2,1)}) %all-gather.5.cloned.1.call-update) | async-done | bytes 1048592 | tf_op jit(solution)/shard_map/all_gather | solution.py:81
  109.8 6.1 conditional.5
  110.0 1.8 gather_fusion
  114.2 1.8 fusion.3
  116.8 93.8 %all-reduce.6.cloned.1.call-done = bf16[128,2048]{1,0:T(8,128)(2,1)} async-done(((bf16[128,2048]{1,0:T(8,128)(2,1)}), bf16[128,2048]{1,0:T(8,128)(2,1)}) %all-reduce.6.cloned.1.call-update) | async-done | bytes 524304 | tf_op jit(solution)/shard_map/psum | solution.py:127
  210.6 1.4 add_convert_fusion.3
  212.0 1.3 collective-permute-start.15
  213.4 1.5 collective-permute-done.15
  214.8 1.2 dynamic-slice_select_fusion.3
  216.0 5.9 conditional.6
  218.2 1.6 fusion.138
  220.0 1.9 fusion.27
  221.9 0.8 copy-done.3
  222.8 95.3 %all-reduce.8.cloned.1.call-done = bf16[128,2048]{1,0:T(8,128)(2,1)} async-done(((bf16[128,2048]{1,0:T(8,128)(2,1)}), bf16[128,2048]{1,0:T(8,128)(2,1)}) %all-reduce.8.cloned.1.call-update) | async-done | bytes 524304 | tf_op jit(solution)/shard_map/psum | solution.py:127
  318.1 1.2 add_convert_fusion.2
  319.3 1.3 collective-permute-start.16
  320.6 1.5 collective-permute-done.16
  322.1 1.2 dynamic-slice_select_fusion.2
  323.3 7.7 %conditional.7 = (bf16[128,2048]{1,0:T(8,128)(2,1)S(1)}) conditional(s32[]{:T(128)} %convert_element_type.212, () %tuple.39, (s32[]{:T(128)}, s32[4,8]{1,0:T(4,128)S(1)}, bf16[16,128,256]{2,1,0:T(8,128)(2,1)S(1)}, s32[4]{0:T(128)S(1)}, bf16[128,2048]{1,0:T(8,128)(2,1)S(1)}, /*index=5*/f32[1,2048]{1,0:T(1,128)S(1)}, ...), branch_computations={%region_13.14_spmd, %region_14.18_spmd} | conditional | flops 204260256 | bytes 7891790 | solution.py:126
  323.4 1.4 gather_fusion.2
  326.2 1.7 fusion.143
  327.9 0.8 copy-done.10
  329.0 2.0 fusion.51
  331.0 0.8 copy-done.4
  331.9 95.4 %all-reduce.10.cloned.1.call-done = bf16[128,2048]{1,0:T(8,128)(2,1)} async-done(((bf16[128,2048]{1,0:T(8,128)(2,1)}), bf16[128,2048]{1,0:T(8,128)(2,1)}) %all-reduce.10.cloned.1.call-update) | async-done | bytes 524304 | tf_op jit(solution)/shard_map/psum | solution.py:127
  427.2 1.2 add_convert_fusion.1
  428.4 2.1 collective-permute-start.17
  430.5 0.8 collective-permute-done.17
  431.4 1.2 dynamic-slice_select_fusion.1
  432.6 7.7 %conditional.8 = (bf16[128,2048]{1,0:T(8,128)(2,1)S(1)}) conditional(s32[]{:T(128)} %convert_element_type.217, () %tuple.41, (s32[]{:T(128)}, s32[4,8]{1,0:T(4,128)S(1)}, bf16[16,128,256]{2,1,0:T(8,128)(2,1)S(1)}, s32[4]{0:T(128)S(1)}, bf16[128,2048]{1,0:T(8,128)(2,1)S(1)}, /*index=5*/f32[1,2048]{1,0:T(1,128)S(1)}, ...), branch_computations={%region_19.20_spmd, %region_20.24_spmd} | conditional | flops 204260256 | bytes 7891790 | solution.py:126
  432.7 1.4 gather_fusion.3
  435.4 1.7 fusion.148
  437.2 0.8 copy-done.11
  438.2 2.0 fusion.75
  440.2 0.8 copy-done.5
  441.1 95.5 %all-reduce.12.cloned.1.call-done = bf16[128,2048]{1,0:T(8,128)(2,1)} async-done(((bf16[128,2048]{1,0:T(8,128)(2,1)}), bf16[128,2048]{1,0:T(8,128)(2,1)}) %all-reduce.12.cloned.1.call-update) | async-done | bytes 524304 | tf_op jit(solution)/shard_map/psum | solution.py:127
  536.6 1.2 add_convert_fusion
  537.8 2.1 collective-permute-start.18
  539.9 0.8 collective-permute-done.18
  540.7 1.2 dynamic-slice_select_fusion
  542.0 0.8 copy-done.6
  542.8 0.8 bitcast_dynamic-update-slice_fusion
  543.7 0.8 fusion.131
  544.5 100.7 %all-reduce.14.cloned.1.call-done = bf16[128,2048]{1,0:T(8,128)(2,1)} async-done(((bf16[128,2048]{1,0:T(8,128)(2,1)}), bf16[128,2048]{1,0:T(8,128)(2,1)}) %all-reduce.14.cloned.1.call-update) | async-done | bytes 524304 | tf_op jit(solution)/shard_map/psum | solution.py:127
  645.2 1.4 fusion.129
  (131 shorter events, 13.0 us)
Async XLA Ops:
  6.5 61.2 %copy-start = (bf16[1,2048,128]{2,1,0:T(8,128)(2,1)S(1)}, bf16[1,2048,128]{2,1,0:T(8,128)(2,1)}, u32[]{:S(2)}) copy-start(bf16[1,2048,128]{2,1,0:T(8,128)(2,1)} %param.28) | copy-start | bytes 1572868
  6.5 63.4 %all-gather.3.cloned.1.call-start = ((), (), s32[]{:S(2)}) async-start(), calls=%async_computation | async-start | bytes 2228224 | tf_op jit(solution)/shard_map/all_gather | solution.py:118
  7.3 102.6 %all-gather.5.cloned.1.call-start = ((), (), s32[]{:S(2)}) async-start(), calls=%async_computation.1 | async-start | bytes 1179648 | tf_op jit(solution)/shard_map/all_gather | solution.py:81
  7.3 4.8 collective-permute-start
  8.9 4.5 collective-permute-start.1
  9.7 58.1 %copy-start.15 = (f32[1,2048]{1,0:T(1,128)S(1)}, f32[1,2048]{1,0:T(1,128)}, u32[]{:S(2)}) copy-start(f32[1,2048]{1,0:T(1,128)} %param.31) | copy-start | bytes 24580
  12.1 7.6 %collective-permute-start.2 = (bf16[256,128]{1,0:T(8,128)(2,1)S(1)}, bf16[256,128]{1,0:T(8,128)(2,1)S(1)}, u32[]{:S(2)}, u32[]{:S(2)}) collective-permute-start(bf16[256,128]{1,0:T(8,128)(2,1)S(1)} %collective-permute-done), channel_id=1, source_target_pairs={{0,8},{8,16},{16,24},{24,32},{32,40},{40,48},{48,56},{56,64},{64,7... | collective-permute-start | bytes 196616 | tf_op jit(solution)/shard_map/ppermute | solution.py:17
  13.4 6.3 collective-permute-start.3
  19.7 8.0 %collective-permute-start.4 = (bf16[256,128]{1,0:T(8,128)(2,1)S(1)}, bf16[256,128]{1,0:T(8,128)(2,1)S(1)}, u32[]{:S(2)}, u32[]{:S(2)}) collective-permute-start(bf16[256,128]{1,0:T(8,128)(2,1)S(1)} %collective-permute-done.2), channel_id=1, source_target_pairs={{0,8},{8,16},{16,24},{24,32},{32,40},{40,48},{48,56},{56,64},{64,7... | collective-permute-start | bytes 196616 | tf_op jit(solution)/shard_map/ppermute | solution.py:17
  19.7 8.0 %collective-permute-start.5 = (bf16[256,128]{1,0:T(8,128)(2,1)S(1)}, bf16[256,128]{1,0:T(8,128)(2,1)S(1)}, u32[]{:S(2)}, u32[]{:S(2)}) collective-permute-start(bf16[256,128]{1,0:T(8,128)(2,1)S(1)} %collective-permute-done.3), channel_id=1, source_target_pairs={{0,120},{8,0},{16,8},{24,16},{32,24},{40,32},{48,40},{56,48},{64,5... | collective-permute-start | bytes 196616 | tf_op jit(solution)/shard_map/ppermute | solution.py:20
  27.7 8.4 %collective-permute-start.6 = (bf16[256,128]{1,0:T(8,128)(2,1)S(1)}, bf16[256,128]{1,0:T(8,128)(2,1)S(1)}, u32[]{:S(2)}, u32[]{:S(2)}) collective-permute-start(bf16[256,128]{1,0:T(8,128)(2,1)S(1)} %collective-permute-done.4), channel_id=1, source_target_pairs={{0,8},{8,16},{16,24},{24,32},{32,40},{40,48},{48,56},{56,64},{64,7... | collective-permute-start | bytes 196616 | tf_op jit(solution)/shard_map/ppermute | solution.py:17
  27.7 8.4 %collective-permute-start.7 = (bf16[256,128]{1,0:T(8,128)(2,1)S(1)}, bf16[256,128]{1,0:T(8,128)(2,1)S(1)}, u32[]{:S(2)}, u32[]{:S(2)}) collective-permute-start(bf16[256,128]{1,0:T(8,128)(2,1)S(1)} %collective-permute-done.5), channel_id=1, source_target_pairs={{0,120},{8,0},{16,8},{24,16},{32,24},{40,32},{48,40},{56,48},{64,5... | collective-permute-start | bytes 196616 | tf_op jit(solution)/shard_map/ppermute | solution.py:20
  36.0 7.4 %collective-permute-start.8 = (bf16[256,128]{1,0:T(8,128)(2,1)S(1)}, bf16[256,128]{1,0:T(8,128)(2,1)S(1)}, u32[]{:S(2)}, u32[]{:S(2)}) collective-permute-start(bf16[256,128]{1,0:T(8,128)(2,1)S(1)} %collective-permute-done.6), channel_id=1, source_target_pairs={{0,8},{8,16},{16,24},{24,32},{32,40},{40,48},{48,56},{56,64},{64,7... | collective-permute-start | bytes 196616 | tf_op jit(solution)/shard_map/ppermute | solution.py:17
  36.0 7.4 %collective-permute-start.9 = (bf16[256,128]{1,0:T(8,128)(2,1)S(1)}, bf16[256,128]{1,0:T(8,128)(2,1)S(1)}, u32[]{:S(2)}, u32[]{:S(2)}) collective-permute-start(bf16[256,128]{1,0:T(8,128)(2,1)S(1)} %collective-permute-done.7), channel_id=1, source_target_pairs={{0,120},{8,0},{16,8},{24,16},{32,24},{40,32},{48,40},{56,48},{64,5... | collective-permute-start | bytes 196616 | tf_op jit(solution)/shard_map/ppermute | solution.py:20
  41.2 27.1 %copy-start.13 = (bf16[1,2048,128]{2,1,0:T(8,128)(2,1)S(1)}, bf16[1,2048,128]{2,1,0:T(8,128)(2,1)}, u32[]{:S(2)}) copy-start(bf16[1,2048,128]{2,1,0:T(8,128)(2,1)} %param.27) | copy-start | bytes 1572868
  43.4 8.7 %collective-permute-start.10 = (bf16[256,128]{1,0:T(8,128)(2,1)S(1)}, bf16[256,128]{1,0:T(8,128)(2,1)S(1)}, u32[]{:S(2)}, u32[]{:S(2)}) collective-permute-start(bf16[256,128]{1,0:T(8,128)(2,1)S(1)} %collective-permute-done.8), channel_id=1, source_target_pairs={{0,8},{8,16},{16,24},{24,32},{32,40},{40,48},{48,56},{56,64},{64,7... | collective-permute-start | bytes 196616 | tf_op jit(solution)/shard_map/ppermute | solution.py:17
  43.4 8.7 %collective-permute-start.11 = (bf16[256,128]{1,0:T(8,128)(2,1)S(1)}, bf16[256,128]{1,0:T(8,128)(2,1)S(1)}, u32[]{:S(2)}, u32[]{:S(2)}) collective-permute-start(bf16[256,128]{1,0:T(8,128)(2,1)S(1)} %collective-permute-done.9), channel_id=1, source_target_pairs={{0,120},{8,0},{16,8},{24,16},{32,24},{40,32},{48,40},{56,48},{64,5... | collective-permute-start | bytes 196616 | tf_op jit(solution)/shard_map/ppermute | solution.py:20
  52.1 8.1 %collective-permute-start.12 = (bf16[256,128]{1,0:T(8,128)(2,1)S(1)}, bf16[256,128]{1,0:T(8,128)(2,1)S(1)}, u32[]{:S(2)}, u32[]{:S(2)}) collective-permute-start(bf16[256,128]{1,0:T(8,128)(2,1)S(1)} %collective-permute-done.10), channel_id=1, source_target_pairs={{0,8},{8,16},{16,24},{24,32},{32,40},{40,48},{48,56},{56,64},{64,7... | collective-permute-start | bytes 196616 | tf_op jit(solution)/shard_map/ppermute | solution.py:17
  52.1 8.1 %collective-permute-start.13 = (bf16[256,128]{1,0:T(8,128)(2,1)S(1)}, bf16[256,128]{1,0:T(8,128)(2,1)S(1)}, u32[]{:S(2)}, u32[]{:S(2)}) collective-permute-start(bf16[256,128]{1,0:T(8,128)(2,1)S(1)} %collective-permute-done.11), channel_id=1, source_target_pairs={{0,120},{8,0},{16,8},{24,16},{32,24},{40,32},{48,40},{56,48},{64,5... | collective-permute-start | bytes 196616 | tf_op jit(solution)/shard_map/ppermute | solution.py:20
  60.2 7.2 %collective-permute-start.14 = (bf16[256,128]{1,0:T(8,128)(2,1)S(1)}, bf16[256,128]{1,0:T(8,128)(2,1)S(1)}, u32[]{:S(2)}, u32[]{:S(2)}) collective-permute-start(bf16[256,128]{1,0:T(8,128)(2,1)S(1)} %collective-permute-done.12), channel_id=1, source_target_pairs={{0,8},{8,16},{16,24},{24,32},{32,40},{40,48},{48,56},{56,64},{64,7... | collective-permute-start | bytes 196616 | tf_op jit(solution)/shard_map/ppermute | solution.py:17
  68.4 41.4 %copy-start.14 = (bf16[1,2048,128]{2,1,0:T(8,128)(2,1)S(1)}, bf16[1,2048,128]{2,1,0:T(8,128)(2,1)}, u32[]{:S(2)}) copy-start(bf16[1,2048,128]{2,1,0:T(8,128)(2,1)} %param.26) | copy-start | bytes 1572868
  68.4 41.4 %copy-start.16 = (f32[1,2048]{1,0:T(1,128)S(1)}, f32[1,2048]{1,0:T(1,128)}, u32[]{:S(2)}) copy-start(f32[1,2048]{1,0:T(1,128)} %param.30) | copy-start | bytes 24580
  68.4 41.4 %copy-start.17 = (s32[4,8]{1,0:T(4,128)S(1)}, s32[4,8]{1,0:T(4,128)}, u32[]{:S(2)}) copy-start(s32[4,8]{1,0:T(4,128)} %param.23) | copy-start | bytes 388
  68.4 41.4 %copy-start.18 = (f32[4,8]{1,0:T(4,128)S(1)}, f32[4,8]{1,0:T(4,128)}, u32[]{:S(2)}) copy-start(f32[4,8]{1,0:T(4,128)} %param.25) | copy-start | bytes 388
  68.4 41.4 %copy-start.19 = (s32[4]{0:T(128)S(1)}, s32[4]{0:T(128)}, u32[]{:S(2)}) copy-start(s32[4]{0:T(128)} %param.24) | copy-start | bytes 52
  69.8 140.8 %all-reduce.6.cloned.1.call-start = ((), (), s32[]{:S(2)}) async-start(), calls=%async_computation.2 | async-start | bytes 1048576 | tf_op jit(solution)/shard_map/psum | solution.py:127
  116.0 0.8 copy-start.2
  116.0 100.0 %copy-start.1 = (bf16[16,128,256]{2,1,0:T(8,128)(2,1)S(1)}, bf16[16,128,256]{2,1,0:T(8,128)(2,1)}, u32[]{:S(2)}) copy-start(bf16[16,128,256]{2,1,0:T(8,128)(2,1)} %all-gather.5.cloned.1.call-done) | copy-start | bytes 3145732
  116.8 201.3 %all-reduce.8.cloned.1.call-start = ((), (), s32[]{:S(2)}) async-start(), calls=%async_computation.3 | async-start | bytes 1048576 | tf_op jit(solution)/shard_map/psum | solution.py:127
  212.0 4.0 copy-start.8
  212.0 2.8 collective-permute-start.15
  216.7 3.1 copy-start.12
  221.9 0.8 copy-start.3
  222.8 204.5 %all-reduce.10.cloned.1.call-start = ((), (), s32[]{:S(2)}) async-start(), calls=%async_computation.4 | async-start | bytes 1048576 | tf_op jit(solution)/shard_map/psum | solution.py:127
  319.3 2.8 collective-permute-start.16
  327.9 0.8 copy-start.10
  331.0 0.8 copy-start.4
  331.8 204.8 %all-reduce.12.cloned.1.call-start = ((), (), s32[]{:S(2)}) async-start(), calls=%async_computation.5 | async-start | bytes 1048576 | tf_op jit(solution)/shard_map/psum | solution.py:127
  428.4 4.1 copy-start.7
  428.4 2.9 collective-permute-start.17
  437.2 0.8 copy-start.11
  440.2 0.8 copy-start.5
  441.0 204.2 %all-reduce.14.cloned.1.call-start = ((), (), s32[]{:S(2)}) async-start(), calls=%async_computation.6 | async-start | bytes 1048576 | tf_op jit(solution)/shard_map/psum | solution.py:127
  537.8 2.9 collective-permute-start.18
  542.0 0.8 copy-start.6
  544.5 100.7 %copy-start.9 = (bf16[1,512,128]{2,1,0:T(8,128)(2,1)}, bf16[1,512,128]{2,1,0:T(8,128)(2,1)S(1)}, u32[]{:S(2)}) copy-start(bf16[1,512,128]{2,1,0:T(8,128)(2,1)S(1)} %fusion.130) | copy-start | bytes 393220
Sparse Core Ops, SparseCore 0:
  9.7 55.9 all-gather.2
  70.0 39.8 all-gather.4
  116.9 93.7 all-reduce.5
  222.9 95.1 all-reduce.7
  332.0 95.2 all-reduce.9
  441.2 95.3 all-reduce.11
  542.9 102.2 all-reduce.13
